TPU v7x, 32 devices: a whole 2x2x4 slice. The times are simulated.
32 devices in a mesh: seg: 2 (over x), smp: 8 (over z, y), snp: 2 (over core).
Axes of the slice: x: 2, y: 2, z: 4, core: 2. Of those that a mesh axis runs over, the one named last changes fastest.
Arguments:
- dosage: bfloat16 [4096, 8192], P('smp', ('seg', 'snp')), parts along dimension 1, may hold values from -48 to 48, as said below
Outputs:
- band_corr: float32 [3, 16, 512, 512], P(None, ('seg', 'snp'), 'smp'), parts along dimension 1
There are 2 independent parts, one for each index of `seg`. A program takes and returns all parts, laid end to end along the dimension named above; each array names one. Nothing has to cross between parts.
Inputs may be any that keep to these rules, and one draw needn't show every extreme that they name: `dosage`: dosages of each SNP share part of their variation with SNPs nearby.
All inputs are finite; a program needn't handle non-finite values.
Results may differ from a plain program's by a relative error of at most 0.0003.
Values may be sent and summed in bfloat16 or wider, within the bound.
No kernel may reach another device: no remote copies, remote signals or barrier semaphores. Data moves between devices by JAX's collectives and lax.ppermute only.
A program may use at most 128 MiB of HBM per device.

v0:
```python
import jax
import jax.numpy as jnp
from jax import lax
from jax.sharding import PartitionSpec as P

BLK = 512


epsilon = 1e-06


def from_behind(x, axis, by):
    length = lax.axis_size(axis)
    pairs = [(i, i + by) for i in range(length) if 0 <= i + by < length]
    return lax.ppermute(x, axis, pairs)


def shards(dosage):
    sample_count = dosage.shape[0]
    block_count = dosage.shape[1] // BLK
    next_cols = from_behind(dosage[:, : 2 * BLK], "snp", -1)
    extended = jnp.concatenate([dosage, next_cols], axis=1)
    own_cube = dosage.reshape(sample_count, block_count, BLK)
    ext_cube = extended.reshape(sample_count, block_count + 2, BLK)

    def make_tiles(right_cube, offsets):
        tile_list = [
            jnp.einsum(
                "hmn,hmq->nmq",
                own_cube,
                right_cube[:, offset : offset + block_count],
                preferred_element_type=jnp.float32,
            )
            for offset in offsets
        ]
        return jnp.stack(tile_list, axis=1)

    tile_rows = BLK // lax.axis_size("smp")
    owned_zero = lax.psum_scatter(
        make_tiles(own_cube, (0,)), "smp", scatter_dimension=0, tiled=True
    )
    owned_band = lax.psum_scatter(
        make_tiles(ext_cube, (1, 2)), "smp", scatter_dimension=0, tiled=True
    )
    owned = jnp.concatenate([owned_zero, owned_band], axis=1)
    gram_tiles = jnp.transpose(owned, (1, 2, 0, 3))
    first_row = lax.axis_index("smp") * tile_rows
    squares = jnp.sum(jnp.square(extended.astype(jnp.float32)), axis=0)
    square_sums = lax.psum(squares, "smp").reshape(block_count + 2, BLK)
    row_sums = lax.dynamic_slice_in_dim(square_sums[:block_count], first_row, tile_rows, 1)
    row_scale = lax.rsqrt(row_sums + epsilon)
    col_scale = lax.rsqrt(square_sums + epsilon)
    col_stack = jnp.stack([col_scale[offset : offset + block_count] for offset in range(3)])
    return gram_tiles * row_scale[None, :, :, None] * col_stack[:, :, None, :]


def solution(mesh):
    return jax.shard_map(
        shards,
        mesh=mesh,
        in_specs=(P("smp", ("seg", "snp")),),
        out_specs=P(None, ("seg", "snp"), "smp", None),
        check_vma=False,
    )
```

profile of v0, /device:TPU:0, one launch (start us, length us, event | category | flops | bytes accessed | tf_op | source)
XLA Modules:
  0.0 457.6 jit_solution(16435303125887998806)
XLA Ops:
  6.5 0.0 all-reduce.5.cloned.1.call-start
  6.5 2.3 slice.35
  8.8 1.3 collective-permute-start
  10.1 5.5 %convolution_bitcast_fusion.2 = f32[512,1,4,512]{0,3,2,1:T(8,128)} fusion(bf16[64,4,8,512]{3,2,1,0:T(8,128)(2,1)} %bitcast.30), kind=kOutput, calls=%fused_computation.4 | convolution fusion | flops 1073741824 | bytes 6291456 | tf_op jit(solution)/shard_map/hmn,hmq->nmq/dot_general | solution.py:28
  15.5 5.4 %copy.18 = f32[512,1,4,512]{3,2,1,0:T(4,128)} copy(f32[512,1,4,512]{0,3,2,1:T(8,128)} %convolution_bitcast_fusion.2) | data formatting | bytes 8388608 | tf_op jit(solution)/shard_map/stack | solution.py:36
  21.0 1.8 constant_dynamic-update-slice_fusion.1
  22.8 0.0 collective-permute-done
  22.8 1.3 constant_dynamic-update-slice_fusion
  24.1 2.8 copy.19
  26.9 0.0 copy-start
  26.9 0.0 copy-start.1
  26.9 3.6 convolution_bitcast_fusion
  30.5 0.0 copy-done
  30.5 0.1 copy-done.1
  30.7 1.3 convolution_bitcast_fusion.1
  31.9 4.3 pad_maximum_fusion
  36.2 10.3 %copy.22 = f32[512,2,4,512]{3,2,1,0:T(4,128)} copy(f32[512,2,4,512]{0,3,2,1:T(8,128)} %pad_maximum_fusion) | data formatting | bytes 16777216 | tf_op jit(solution)/shard_map/stack | solution.py:36
  46.5 0.0 copy-start.2
  46.5 0.0 all-reduce.5.cloned.1.call-update
  46.5 0.6 copy-done.2
  47.1 0.6 dynamic-slice
  48.4 0.7 multiply_reduce_fusion
  49.1 41.2 %psum.7 = f32[3072]{0:T(1024)S(1)} all-reduce(f32[3072]{0:T(1024)S(1)} %multiply_reduce_fusion), channel_id=1, replica_groups=mesh['seg'=2,'smp'=8,'snp'=2] {'smp'}, use_global_device_ids=true, to_apply=%region_3.0 | all-reduce | flops 3072 | bytes 24576 | tf_op jit(solution)/shard_map/psum | solution.py:49
  90.3 0.1 add_rsqrt_fusion.1
  90.4 0.1 copy.23
  90.5 355.9 %all-reduce.5.cloned.1.call-done = (f32[512,2,4,512]{3,2,1,0:T(4,128)}, f32[512,1,4,512]{3,2,1,0:T(4,128)}) async-done(((f32[512,2,4,512]{3,2,1,0:T(4,128)}, f32[512,1,4,512]{3,2,1,0:T(4,128)}), (f32[512,2,4,512]{3,2,1,0:T(4,128)}, f32[512,1,4,512]{3,2,1,0:T(4,128)})) %all-reduce.5.cloned.1.call-update) | async-done | bytes 12582928
  446.4 1.3 constant_dynamic-slice_fusion
  447.7 1.1 constant_dynamic-slice_fusion.1
  448.8 0.4 fusion.7
  449.2 1.6 copy.24
  (8 shorter events, 0.1 us)
Async XLA Ops:
  6.5 439.8 %all-reduce.5.cloned.1.call-start = ((), (), s32[]{:S(2)}) async-start(), calls=%async_computation | async-start | bytes 25165824
  8.8 14.0 %collective-permute-start = (bf16[512,1024]{1,0:T(8,128)(2,1)}, bf16[512,1024]{1,0:T(8,128)(2,1)}, u32[]{:S(2)}, u32[]{:S(2)}) collective-permute-start(bf16[512,1024]{1,0:T(8,128)(2,1)} %slice.35), channel_id=1, source_target_pairs={{1,0},{3,2},{5,4},{7,6},{9,8},{11,10},{13,12},{15,14},{17,16},{19,... | collective-permute-start | bytes 3145736 | tf_op jit(solution)/shard_map/ppermute | solution.py:15
  26.9 3.6 copy-start
  26.9 3.8 copy-start.1
  46.5 0.7 copy-start.2
Sparse Core Ops, SparseCore 0:
  46.6 399.6 all-reduce.4
where the time goes:
time: 458 us
  waiting for transfers between devices  356 us (78%)
  blocking collectives  41.2 us (9%)
  local copies, waits for them, and re-layouts  29.3 us (6%)
  between operations  14.1 us (3%)
  matrix products  10.4 us (2%)
  other arithmetic  5.45 us (1%)
    unnamed x2, waiting for transfers between devices  356 us
    psum x1, blocking collectives, shards(): square_sums = lax.psum(squares, 'smp').reshape(block_count + 2, BLK)  41.2 us
    another operation x2, local copies, waits for them, and re-layouts, make_tiles(): return jnp.stack(tile_list, axis=1)  15.7 us
    dot_general x3, matrix products, make_tiles(): jnp.einsum('hmn,hmq->nmq', own_cube, right_cube[:, offset:offset + block_...  10.4 us
  transfers between devices with their start and end apart: 2, of which 1 were waited for; matrix products, arithmetic and copies ran while one was open for 3% of the time, Pallas kernels for 0%

commit v1 on v0

v1 whole, which is shorter than its diff:
```python
import functools

import jax
import jax.numpy as jnp
from jax import lax
from jax.experimental import pallas as pl
from jax.experimental.pallas import tpu as pltpu
from jax.sharding import PartitionSpec as P


BLK = 512
LANES = 128
EPS = 1e-06
BOOST = 2.0**15
F32 = jnp.float32
F16 = jnp.float16
BF16 = jnp.bfloat16
VM = pl.BlockSpec(memory_space=pltpu.VMEM)
PARAMS = pltpu.CompilerParams(vmem_limit_bytes=16 * 2**20)
ANY = pl.BlockSpec(memory_space=pl.ANY)


def mm(lt, right):
    return jnp.dot(lt, right, preferred_element_type=F32)


def vm(x):
    return pltpu.with_memory_space_constraint(x, pltpu.VMEM)


def odd_core():
    return lax.rem(lax.axis_index("snp"), 2)


def block_at(nb, t):
    return jnp.where(odd_core() == 0, nb - 1 - t, t)


def prep_kernel(nb, d_ref, *refs):
    outs, sq_ref, sems = refs[:nb], refs[nb], refs[nb + 1]
    copies = []
    for t in range(nb):
        begin = pl.multiple_of(block_at(nb, t) * BLK, BLK)
        copies.append(pltpu.make_async_copy(d_ref.at[:, pl.ds(begin, BLK)], outs[t], sems.at[t]))
        copies[t].start()
    for t in range(nb):
        copies[t].wait()
        f = outs[t][...].astype(F32)
        sq_ref[t : t + 1, :] = jnp.sum(f * f, axis=0, keepdims=True)


def put_rows(x, wide, dst, flip=0):
    me = lax.axis_index("smp")
    z, half = me // 2, lax.rem(me, 2) ^ flip
    wide[...] = x.T.reshape(wide.shape)
    for rel in range(wide.shape[0]):
        dst[rel] = wide[z ^ rel, half]


def rows_kernel(nb, *refs):
    ins, out, wide = refs[:nb], refs[nb], refs[nb + 1]
    for t in range(nb):
        put_rows(ins[t][...], wide.at[t], out.at[t])


def scale_kernel(a_ref, b_ref, col_ref, first_ref, rows_ref, flip_ref, wide):
    scale = lax.rsqrt(a_ref[...] + b_ref[...] + EPS)
    col_ref[...] = scale
    first_ref[...] = scale[:2]
    for t in range(a_ref.shape[0]):
        put_rows(jnp.broadcast_to(scale[t : t + 1] * BOOST, (LANES, BLK)), wide.at[t], rows_ref.at[t])
    put_rows(jnp.broadcast_to(scale[t : t + 1] * BOOST, (LANES, BLK)), wide.at[t], flip_ref, 1)


def emit(keep, send, m, acc, row, col):
    count, _, tr, _ = keep.shape
    acc = acc * col
    for i in range(BLK // LANES):
        part = (acc[:, i * LANES : (i + 1) * LANES] * row).reshape(count, 2, tr, LANES)
        keep[:, m, :, i * LANES : (i + 1) * LANES] = part[:, 0]
        send[:, m, :, i * LANES : (i + 1) * LANES] = part[:, 1]


def flat(x):
    return x.reshape(x.shape[0] * x.shape[1], x.shape[2])


def chunk_kernel(t, ms, new, cols, rows_ref, lown_ref, *refs):
    k = max(ms) + 1
    own, other = refs[:k], refs[k : 2 * k]
    if new:
        lother = refs[2 * k : 3 * k - 1]
        keep, send, lnew, wide = refs[3 * k - 1 :]
        put_rows(other[0][...], wide, lnew)
        lother = (lnew,) + tuple(lother)
    else:
        lother = refs[2 * k : 3 * k]
        keep, send = refs[3 * k :]

    def even():
        lo, lr = flat(lown_ref[t]), flat(lother[0][...])
        row = flat(rows_ref[t])
        for i, m in enumerate(ms):
            acc = mm(lo, own[m][...]) + mm(lr, other[m][...])
            emit(keep, send, i, acc, row, cols[t - m : t - m + 1, :])

    def uneven():
        ro, rr = own[0][...], other[0][...]
        col = cols[t : t + 1, :]
        for i, m in enumerate(ms):
            acc = mm(flat(lown_ref[t - m]), ro) + mm(flat(lother[m][...]), rr)
            emit(keep, send, i, acc, flat(rows_ref[t - m]), col)

    pl.when(odd_core() == 0)(even)
    pl.when(odd_core() != 0)(uneven)


def own_kernel(cols, rows_ref, flip_ref, lown_ref, own, keep, send, flipped, wide):
    t = cols.shape[0] - 1
    put_rows(own[...], wide, flipped, 1)
    for i, (lt, row) in enumerate(((lown_ref[t], rows_ref[t]), (flipped[...], flip_ref[...]))):
        emit(keep, send, i, mm(flat(lt), own[...]), flat(row), cols[t : t + 1, :])


HALO = ((1, 0, 0), (2, 0, 1), (2, 1, 0))


def halo_kernel(cores, cols, rows_ref, lown_ref, l0, l1, o0, o1, r0, r1, keep, send):
    last = lax.axis_index("snp") == cores - 1

    @pl.when(jnp.logical_not(last))
    def _():
        for m, (_, a, b) in enumerate(HALO):
            acc = mm(flat(lown_ref[a]), (o0, o1)[b][...]) + mm(flat((l0, l1)[a][...]), (r0, r1)[b][...])
            emit(keep, send, m, acc, flat(rows_ref[a]), cols[b : b + 1, :])

    @pl.when(last)
    def _():
        keep[...] = jnp.zeros_like(keep)
        send[...] = jnp.zeros_like(send)


def place_kernel(nb, names, *refs):
    tiles, out, sems = refs[: len(names)], refs[-2], refs[-1]
    copies = []
    for name, tile in zip(names, tiles):
        for i in range(tile.shape[0]):
            if name == "h":
                dst = out.at[HALO[i][0], nb - 1 - HALO[i][1]]
            else:
                t, m = name[0], name[1][i]
                dst = out.at[m, jnp.where(odd_core() == 0, nb - 1 - t, t - m)]
            copies.append(pltpu.make_async_copy(tile.at[i], dst, sems.at[len(copies)]))
    for c in copies:
        c.start()
    for c in copies:
        c.wait()


def kernel_call(body, out_shape, args, scratch=()):
    vmem_out = [pltpu.VMEM(s, t) for s, t in out_shape]
    return pl.pallas_call(
        body,
        out_shape=vmem_out,
        in_specs=[VM] * len(args),
        out_specs=[VM] * len(vmem_out),
        scratch_shapes=list(scratch),
        compiler_params=PARAMS,
    )(*[vm(a) for a in args])


def shards(n, cores, dosage):
    samples, width = dosage.shape
    nb = width // BLK
    tr = BLK // n
    zs = n // 2
    bits = [1 << b for b in range(1, n.bit_length() - 1)]

    def swap(x, bit, only=None):
        if only is None:
            return lax.ppermute(x, "smp", [(i, i ^ bit) for i in range(n)])
        return lax.ppermute(x, ("smp", "snp"), [(i * cores + c, (i ^ bit) * cores + c) for i in range(n) for c in only])

    def from_next(x):
        return lax.ppermute(x, "snp", [(c + 1, c) for c in range(cores - 1)])

    *own, squares = pl.pallas_call(
        functools.partial(prep_kernel, nb),
        out_shape=[pltpu.VMEM((samples, BLK), BF16)] * nb + [pltpu.VMEM((nb, BLK), F32)],
        in_specs=[ANY],
        out_specs=[VM] * (nb + 1),
        scratch_shapes=[pltpu.SemaphoreType.DMA((nb,))],
        compiler_params=PARAMS,
    )(dosage)
    got = swap(squares, 1)
    other = [swap(own[t], 1) for t in range(nb)]
    halo_own = [from_next(own[t]) for t in range(2)]
    lown = kernel_call(functools.partial(rows_kernel, nb), [((nb, zs, tr, samples), BF16)], own, [pltpu.VMEM((nb, zs, 2, tr, samples), BF16)])[0]
    for bit in bits:
        squares = squares + got
        got = swap(squares, bit)
    cols, first, rows, flip = kernel_call(
        scale_kernel,
        [((nb, BLK), F32), ((2, BLK), F32), ((nb, zs, tr, LANES), F32), ((zs, tr, LANES), F32)],
        [squares, got],
        [pltpu.VMEM((nb, zs, 2, tr, LANES), F32)],
    )
    halo_cols = from_next(first)

    def reduce(name, keep, send, only=None):
        terms = [keep, swap(send.astype(F16), bits[0], only)]
        for bit in bits[1:]:
            sent = sum(x[1::2].astype(F32) for x in terms).astype(F16)
            terms = [x[0::2] for x in terms] + [swap(sent, bit, only)]
        if name == "e":
            sent = sum(x[0, 1:].astype(F32) for x in terms).astype(F16)
            terms = [x[:, :1] for x in terms] + [swap(sent, 1)[None]]
        return sum(x[0].astype(F32) for x in terms) * (1.0 / BOOST)

    def place(out, tiles, names):
        count = sum(t.shape[0] for t in tiles)
        extra = [] if out is None else [out]
        return pl.pallas_call(
            functools.partial(place_kernel, nb, names),
            out_shape=jax.ShapeDtypeStruct((3, nb, tr, BLK), F32),
            in_specs=[VM] * len(tiles) + [ANY] * len(extra),
            out_specs=ANY,
            scratch_shapes=[pltpu.SemaphoreType.DMA((count,))],
            compiler_params=PARAMS,
            input_output_aliases={len(tiles): 0} if extra else {},
        )(*[vm(t) for t in tiles], *extra)

    lother = []
    keep, send, _ = kernel_call(
        own_kernel,
        [((zs // 2, 2, tr, BLK), F32)] * 2 + [((zs, tr, samples), BF16)],
        [cols, rows, flip, lown, own[nb - 1]],
        [pltpu.VMEM((zs, 2, tr, samples), BF16)],
    )
    parts = {(nb - 1, (0,)): ("e", keep, send)}
    for t in range(nb):
        for g, ms in enumerate(groups_of(t)):
            k = max(ms) + 1
            keep, send, *lnew = kernel_call(
                functools.partial(chunk_kernel, t, ms, g == 0),
                [((zs // 2, len(ms), tr, BLK), F32)] * 2 + [((zs, tr, samples), BF16)] * (g == 0),
                [cols, rows, lown] + [own[t - j] for j in range(k)] + [other[t - j] for j in range(k)] + [lother[t - j] for j in range(g == 0, k)],
                [pltpu.VMEM((zs, 2, tr, samples), BF16)] * (g == 0),
            )
            lother += lnew
            parts[t, ms] = (f"c{t}{g}", keep, send)
        if t == 1:
            halo_other = [from_next(other[j]) for j in range(2)]
            keep, send = kernel_call(
                functools.partial(halo_kernel, cores),
                [((zs // 2, len(HALO), tr, BLK), F32)] * 2,
                [halo_cols, rows, lown, lother[0], lother[1], *halo_own, *halo_other],
            )
            parts["h"] = ("h", keep, send, range(cores - 1))
    tiles = {key: reduce(*part) for key, part in parts.items()}
    final = (nb - 1, groups_of(nb - 1)[-1])
    early = [key for key in tiles if key != final]
    out = place(None, [tiles[key] for key in early], early)
    return place(out, [tiles[final]], [final])


def groups_of(t):
    return (((0,),), ((0, 1),), ((0, 1), (2,)), ((1,), (2,)))[t]


def solution(mesh):
    n, cores = mesh.shape["smp"], mesh.shape["snp"]

    def body(dosage):
        return shards(n, cores, dosage)

    return jax.shard_map(
        body,
        mesh=mesh,
        in_specs=(P("smp", ("seg", "snp")),),
        out_specs=P(None, ("seg", "snp"), "smp", None),
        check_vma=False,
    )
```

time: 458 us -> 129 us (0.28)
  waiting for transfers between devices: 356 us -> 60.3 us
  starting transfers between devices: 1.28 us -> 56.3 us
  blocking collectives: 41.2 us -> 0 us
  local copies, waits for them, and re-layouts: 29.3 us -> 1.59 us
  between operations: 14.1 us -> 0.36 us
  matrix products: 10.4 us -> 0 us
  Pallas kernels: 0 us -> 9.43 us
    unnamed x2 -> x0, waiting for transfers between devices: 356 us -> none
    ppermute x1 -> x29, waiting for transfers between devices: 0.01 us -> 60.3 us  [the longest x22 50.5 us: swap(): return lax.ppermute(x, 'smp', [(i, i ^ bit) for i in range(n)])]
    ppermute x1 -> x29, starting transfers between devices: 1.28 us -> 56.3 us  [the longest x22 43.8 us: swap(): return lax.ppermute(x, 'smp', [(i, i ^ bit) for i in range(n)])]
    psum x1 -> x0, blocking collectives: 41.2 us -> none  [shards(): square_sums = lax.psum(squares, 'smp').reshape(block_count + 2, BLK)]
    another operation x5 -> x0, local copies, waits for them, and re-layouts: 15.7 us -> none  [the longest x2 15.7 us: make_tiles(): return jnp.stack(tile_list, axis=1)]
    dot_general x3 -> x0, matrix products: 10.4 us -> none  [make_tiles(): jnp.einsum('hmn,hmq->nmq', own_cube, right_cube[:, offset:offset + block_...]
    pallas_call x0 -> x13, Pallas kernels: none -> 9.43 us  [the longest x10 7 us: kernel_call(): pl.pallas_call(body, out_shape=vmem_out, in_specs=[VM] * len(args), out_s...]
  transfers between devices with their start and end apart: 2 -> 29, of which waited for: 1 -> 14; matrix products, arithmetic and copies ran while one was open for 3% -> 1% of each run, Pallas kernels for 0% -> 4%
where the time goes in v1:
time: 129 us
  waiting for transfers between devices  60.3 us (47%)
  starting transfers between devices  56.3 us (44%)
  Pallas kernels  9.43 us (7%)
  local copies, waits for them, and re-layouts  1.59 us (1%)
    ppermute x22, waiting for transfers between devices, swap(): return lax.ppermute(x, 'smp', [(i, i ^ bit) for i in range(n)])  50.5 us
    ppermute x22, starting transfers between devices, swap(): return lax.ppermute(x, 'smp', [(i, i ^ bit) for i in range(n)])  43.8 us
    ppermute x2, waiting for transfers between devices, swap(): lax.ppermute(x, ('smp', 'snp'), [(i * cores + c, (i ^ bit) * cores + c) f...  9.81 us
    pallas_call x10, Pallas kernels, kernel_call(): pl.pallas_call(body, out_shape=vmem_out, in_specs=[VM] * len(args), out_s...  7 us
    ppermute x5, starting transfers between devices, from_next(): return lax.ppermute(x, 'snp', [(c + 1, c) for c in range(cores - 1)])  6.44 us
    ppermute x2, starting transfers between devices, swap(): lax.ppermute(x, ('smp', 'snp'), [(i * cores + c, (i ^ bit) * cores + c) f...  6.02 us
  transfers between devices with their start and end apart: 29, of which 14 were waited for; matrix products, arithmetic and copies ran while one was open for 1% of the time, Pallas kernels for 4%

profile of v1, /device:TPU:0, one launch (start us, length us, event | category | flops | bytes accessed | tf_op | source)
XLA Modules:
  0.0 128.9 jit_solution(1515421076213230662)
XLA Ops:
  0.0 1.6 %copy-done = bf16[512,2048]{1,0:T(8,128)(2,1)S(1)} copy-done((bf16[512,2048]{1,0:T(8,128)(2,1)S(1)}, bf16[512,2048]{1,0:T(8,128)(2,1)}, u32[]{:S(2)}) %copy-start) | copy-done | bytes 2097176
  1.6 0.6 shard_map.17
  2.2 3.1 %collective-permute-start = (f32[4,512]{1,0:T(4,128)S(1)}, f32[4,512]{1,0:T(4,128)S(1)}, u32[]{:S(2)}, u32[]{:S(2)}) collective-permute-start(f32[4,512]{1,0:T(4,128)S(1)} %get-tuple-element.34), channel_id=1, source_target_pairs={{0,2},{2,0},{4,6},{6,4},{8,10},{10,8},{12,14},{14,12},{1,3},{3,1},... | collective-permute-start | bytes 24584 | tf_op jit(solution)/shard_map/ppermute | solution.py:181
  5.2 1.6 %collective-permute-done = f32[4,512]{1,0:T(4,128)S(1)} collective-permute-done((f32[4,512]{1,0:T(4,128)S(1)}, f32[4,512]{1,0:T(4,128)S(1)}, u32[]{:S(2)}, u32[]{:S(2)}) %collective-permute-start) | collective-permute-done | bytes 8224 | tf_op jit(solution)/shard_map/ppermute | solution.py:181
  6.9 2.1 %collective-permute-start.1 = (f32[4,512]{1,0:T(4,128)S(1)}, f32[4,512]{1,0:T(4,128)S(1)}, u32[]{:S(2)}, u32[]{:S(2)}) collective-permute-start(f32[4,512]{1,0:T(4,128)S(1)} %add.203), channel_id=1, source_target_pairs={{0,4},{2,6},{4,0},{6,2},{8,12},{10,14},{12,8},{14,10},{1,5},{3,7},... | collective-permute-start | bytes 24584 | tf_op jit(solution)/shard_map/ppermute | solution.py:181
  8.9 1.6 %collective-permute-done.1 = f32[4,512]{1,0:T(4,128)S(1)} collective-permute-done((f32[4,512]{1,0:T(4,128)S(1)}, f32[4,512]{1,0:T(4,128)S(1)}, u32[]{:S(2)}, u32[]{:S(2)}) %collective-permute-start.1) | collective-permute-done | bytes 8224 | tf_op jit(solution)/shard_map/ppermute | solution.py:181
  10.6 3.0 %collective-permute-start.2 = (f32[4,512]{1,0:T(4,128)S(1)}, f32[4,512]{1,0:T(4,128)S(1)}, u32[]{:S(2)}, u32[]{:S(2)}) collective-permute-start(f32[4,512]{1,0:T(4,128)S(1)} %add.204.a_ref), channel_id=1, source_target_pairs={{0,8},{2,10},{4,12},{6,14},{8,0},{10,2},{12,4},{14,6},{1,9},{3,11}... | collective-permute-start | bytes 24584 | tf_op jit(solution)/shard_map/ppermute | solution.py:181
  13.6 0.6 shard_map.19.lown_ref
  14.2 1.0 collective-permute-done.2.b_ref
  15.2 0.4 shard_map.18
  15.6 1.0 shard_map.25
  16.6 2.0 %collective-permute-start.9 = (f16[2,2,64,512]{3,2,1,0:T(8,128)(2,1)S(1)}, f16[2,2,64,512]{3,2,1,0:T(8,128)(2,1)S(1)}, u32[]{:S(2)}, u32[]{:S(2)}) collective-permute-start(f16[2,2,64,512]{3,2,1,0:T(8,128)(2,1)S(1)} %convert_element_type.262), channel_id=1, source_target_pairs={{0,4},{2,6},{4,0},{6,2},{8,12},{10,14},{12,8},{14,10},{1,5},{3,7},... | collective-permute-start | bytes 786440 | tf_op jit(solution)/shard_map/ppermute | solution.py:181
  18.6 1.5 %collective-permute-start.6 = (bf16[512,512]{1,0:T(8,128)(2,1)S(1)}, bf16[512,512]{1,0:T(8,128)(2,1)S(1)}, u32[]{:S(2)}, u32[]{:S(2)}) collective-permute-start(bf16[512,512]{1,0:T(8,128)(2,1)S(1)} %get-tuple-element.37.refs_0_.refs_1_.refs_2_), channel_id=1, source_target_pairs={{0,2},{2,0},{4,6},{6,4},{8,10},{10,8},{12,14},{14,12},{1,3},{3,1},... | collective-permute-start | bytes 1572872 | tf_op jit(solution)/shard_map/ppermute | solution.py:181
  20.1 4.3 %collective-permute-done.9 = f16[2,2,64,512]{3,2,1,0:T(8,128)(2,1)S(1)} collective-permute-done((f16[2,2,64,512]{3,2,1,0:T(8,128)(2,1)S(1)}, f16[2,2,64,512]{3,2,1,0:T(8,128)(2,1)S(1)}, u32[]{:S(2)}, u32[]{:S(2)}) %collective-permute-start.9) | collective-permute-done | bytes 262176 | tf_op jit(solution)/shard_map/ppermute | solution.py:181
  24.5 3.0 %collective-permute-start.10 = (f16[1,2,64,512]{3,2,1,0:T(8,128)(2,1)S(1)}, f16[1,2,64,512]{3,2,1,0:T(8,128)(2,1)S(1)}, u32[]{:S(2)}, u32[]{:S(2)}) collective-permute-start(f16[1,2,64,512]{3,2,1,0:T(8,128)(2,1)S(1)} %add_convert_fusion.3), channel_id=1, source_target_pairs={{0,8},{2,10},{4,12},{6,14},{8,0},{10,2},{12,4},{14,6},{1,9},{3,11}... | collective-permute-start | bytes 393224 | tf_op jit(solution)/shard_map/ppermute | solution.py:181
  27.5 1.5 %collective-permute-start.3 = (bf16[512,512]{1,0:T(8,128)(2,1)S(1)}, bf16[512,512]{1,0:T(8,128)(2,1)S(1)}, u32[]{:S(2)}, u32[]{:S(2)}) collective-permute-start(bf16[512,512]{1,0:T(8,128)(2,1)S(1)} %get-tuple-element.40.refs_3_.refs_0_.own), channel_id=1, source_target_pairs={{0,2},{2,0},{4,6},{6,4},{8,10},{10,8},{12,14},{14,12},{1,3},{3,1},... | collective-permute-start | bytes 1572872 | tf_op jit(solution)/shard_map/ppermute | solution.py:181
  29.0 0.5 collective-permute-start.4
  29.5 1.5 %collective-permute-start.5 = (bf16[512,512]{1,0:T(8,128)(2,1)S(1)}, bf16[512,512]{1,0:T(8,128)(2,1)S(1)}, u32[]{:S(2)}, u32[]{:S(2)}) collective-permute-start(bf16[512,512]{1,0:T(8,128)(2,1)S(1)} %get-tuple-element.38.refs_1_.refs_0_.refs_2_), channel_id=1, source_target_pairs={{0,2},{2,0},{4,6},{6,4},{8,10},{10,8},{12,14},{14,12},{1,3},{3,1},... | collective-permute-start | bytes 1572872 | tf_op jit(solution)/shard_map/ppermute | solution.py:181
  31.0 0.8 collective-permute-done.10
  31.9 1.9 %collective-permute-start.11 = (f16[1,64,512]{2,1,0:T(8,128)(2,1)S(1)}, f16[1,64,512]{2,1,0:T(8,128)(2,1)S(1)}, u32[]{:S(2)}, u32[]{:S(2)}) collective-permute-start(f16[1,64,512]{2,1,0:T(8,128)(2,1)S(1)} %fusion.1), channel_id=1, source_target_pairs={{0,2},{2,0},{4,6},{6,4},{8,10},{10,8},{12,14},{14,12},{1,3},{3,1},... | collective-permute-start | bytes 196616 | tf_op jit(solution)/shard_map/ppermute | solution.py:181
  33.8 0.0 collective-permute-done.6.refs_1_.refs_3_.refs_5_
  33.8 1.3 collective-permute-start.17
  35.1 0.6 shard_map.20
  35.8 27.9 %collective-permute-done.11 = f16[1,64,512]{2,1,0:T(8,128)(2,1)S(1)} collective-permute-done((f16[1,64,512]{2,1,0:T(8,128)(2,1)S(1)}, f16[1,64,512]{2,1,0:T(8,128)(2,1)S(1)}, u32[]{:S(2)}, u32[]{:S(2)}) %collective-permute-start.11) | collective-permute-done | bytes 65568 | tf_op jit(solution)/shard_map/ppermute | solution.py:181
  63.6 0.4 collective-permute-start.12
  64.1 1.3 %collective-permute-start.16 = (f32[2,512]{1,0:T(2,128)S(1)}, f32[2,512]{1,0:T(2,128)S(1)}, u32[]{:S(2)}, u32[]{:S(2)}) collective-permute-start(f32[2,512]{1,0:T(2,128)S(1)} %get-tuple-element.54), channel_id=1, source_target_pairs={{1,0},{3,2},{5,4},{7,6},{9,8},{11,10},{13,12},{15,14},{17,16},{19,... | collective-permute-start | bytes 12296 | tf_op jit(solution)/shard_map/ppermute | solution.py:185
  65.4 0.9 shard_map.21
  66.4 0.0 collective-permute-done.4.refs_2_.refs_3_.refs_4_
  66.4 1.7 %collective-permute-start.14 = (f16[2,2,64,512]{3,2,1,0:T(8,128)(2,1)S(1)}, f16[2,2,64,512]{3,2,1,0:T(8,128)(2,1)S(1)}, u32[]{:S(2)}, u32[]{:S(2)}) collective-permute-start(f16[2,2,64,512]{3,2,1,0:T(8,128)(2,1)S(1)} %convert_element_type.277), channel_id=1, source_target_pairs={{0,4},{2,6},{4,0},{6,2},{8,12},{10,14},{12,8},{14,10},{1,5},{3,7},... | collective-permute-start | bytes 786440 | tf_op jit(solution)/shard_map/ppermute | solution.py:181
  68.1 0.9 shard_map.22
  69.0 0.5 shard_map.27
  69.5 0.5 collective-permute-start.25
  70.0 0.6 shard_map.23
  70.7 0.5 shard_map.24
  71.2 1.7 %collective-permute-start.27 = (f16[2,1,64,512]{3,2,1,0:T(8,128)(2,1)S(1)}, f16[2,1,64,512]{3,2,1,0:T(8,128)(2,1)S(1)}, u32[]{:S(2)}, u32[]{:S(2)}) collective-permute-start(f16[2,1,64,512]{3,2,1,0:T(8,128)(2,1)S(1)} %convert_element_type.297), channel_id=1, source_target_pairs={{0,4},{2,6},{4,0},{6,2},{8,12},{10,14},{12,8},{14,10},{1,5},{3,7},... | collective-permute-start | bytes 393224 | tf_op jit(solution)/shard_map/ppermute | solution.py:181
  72.9 5.4 %collective-permute-done.25 = f16[2,1,64,512]{3,2,1,0:T(8,128)(2,1)S(1)} collective-permute-done((f16[2,1,64,512]{3,2,1,0:T(8,128)(2,1)S(1)}, f16[2,1,64,512]{3,2,1,0:T(8,128)(2,1)S(1)}, u32[]{:S(2)}, u32[]{:S(2)}) %collective-permute-start.25) | collective-permute-done | bytes 131104 | tf_op jit(solution)/shard_map/ppermute | solution.py:181
  78.3 1.6 %collective-permute-start.7 = (f16[2,1,64,512]{3,2,1,0:T(8,128)(2,1)S(1)}, f16[2,1,64,512]{3,2,1,0:T(8,128)(2,1)S(1)}, u32[]{:S(2)}, u32[]{:S(2)}) collective-permute-start(f16[2,1,64,512]{3,2,1,0:T(8,128)(2,1)S(1)} %convert_element_type.257), channel_id=1, source_target_pairs={{0,4},{2,6},{4,0},{6,2},{8,12},{10,14},{12,8},{14,10},{1,5},{3,7},... | collective-permute-start | bytes 393224 | tf_op jit(solution)/shard_map/ppermute | solution.py:181
  79.9 1.2 collective-permute-done.27
  81.1 2.6 %collective-permute-start.13 = (f16[1,1,64,512]{3,2,1,0:T(8,128)(2,1)S(1)}, f16[1,1,64,512]{3,2,1,0:T(8,128)(2,1)S(1)}, u32[]{:S(2)}, u32[]{:S(2)}) collective-permute-start(f16[1,1,64,512]{3,2,1,0:T(8,128)(2,1)S(1)} %add_convert_fusion.6), channel_id=1, source_target_pairs={{0,8},{2,10},{4,12},{6,14},{8,0},{10,2},{12,4},{14,6},{1,9},{3,11}... | collective-permute-start | bytes 196616 | tf_op jit(solution)/shard_map/ppermute | solution.py:181
  83.8 0.3 collective-permute-done.7
  84.1 3.1 %collective-permute-start.26 = (f16[1,1,64,512]{3,2,1,0:T(8,128)(2,1)S(1)}, f16[1,1,64,512]{3,2,1,0:T(8,128)(2,1)S(1)}, u32[]{:S(2)}, u32[]{:S(2)}) collective-permute-start(f16[1,1,64,512]{3,2,1,0:T(8,128)(2,1)S(1)} %add_convert_fusion.5), channel_id=1, source_target_pairs={{0,8},{2,10},{4,12},{6,14},{8,0},{10,2},{12,4},{14,6},{1,9},{3,11}... | collective-permute-start | bytes 196616 | tf_op jit(solution)/shard_map/ppermute | solution.py:181
  87.2 1.7 %collective-permute-start.28 = (f16[1,1,64,512]{3,2,1,0:T(8,128)(2,1)S(1)}, f16[1,1,64,512]{3,2,1,0:T(8,128)(2,1)S(1)}, u32[]{:S(2)}, u32[]{:S(2)}) collective-permute-start(f16[1,1,64,512]{3,2,1,0:T(8,128)(2,1)S(1)} %add_convert_fusion.4), channel_id=1, source_target_pairs={{0,8},{2,10},{4,12},{6,14},{8,0},{10,2},{12,4},{14,6},{1,9},{3,11}... | collective-permute-start | bytes 196616 | tf_op jit(solution)/shard_map/ppermute | solution.py:181
  88.9 1.7 %collective-permute-done.26 = f16[1,1,64,512]{3,2,1,0:T(8,128)(2,1)S(1)} collective-permute-done((f16[1,1,64,512]{3,2,1,0:T(8,128)(2,1)S(1)}, f16[1,1,64,512]{3,2,1,0:T(8,128)(2,1)S(1)}, u32[]{:S(2)}, u32[]{:S(2)}) %collective-permute-start.26) | collective-permute-done | bytes 65568 | tf_op jit(solution)/shard_map/ppermute | solution.py:181
  90.6 2.3 %collective-permute-start.8 = (f16[1,1,64,512]{3,2,1,0:T(8,128)(2,1)S(1)}, f16[1,1,64,512]{3,2,1,0:T(8,128)(2,1)S(1)}, u32[]{:S(2)}, u32[]{:S(2)}) collective-permute-start(f16[1,1,64,512]{3,2,1,0:T(8,128)(2,1)S(1)} %add_convert_fusion.8), channel_id=1, source_target_pairs={{0,8},{2,10},{4,12},{6,14},{8,0},{10,2},{12,4},{14,6},{1,9},{3,11}... | collective-permute-start | bytes 196616 | tf_op jit(solution)/shard_map/ppermute | solution.py:181
  93.0 1.3 %collective-permute-start.18 = (bf16[512,512]{1,0:T(8,128)(2,1)S(1)}, bf16[512,512]{1,0:T(8,128)(2,1)S(1)}, u32[]{:S(2)}, u32[]{:S(2)}) collective-permute-start(bf16[512,512]{1,0:T(8,128)(2,1)S(1)} %get-tuple-element.38.refs_1_.refs_0_.refs_2_), channel_id=1, source_target_pairs={{1,0},{3,2},{5,4},{7,6},{9,8},{11,10},{13,12},{15,14},{17,16},{19,... | collective-permute-start | bytes 1572872 | tf_op jit(solution)/shard_map/ppermute | solution.py:185
  94.3 1.3 %collective-permute-start.19 = (bf16[512,512]{1,0:T(8,128)(2,1)S(1)}, bf16[512,512]{1,0:T(8,128)(2,1)S(1)}, u32[]{:S(2)}, u32[]{:S(2)}) collective-permute-start(bf16[512,512]{1,0:T(8,128)(2,1)S(1)} %collective-permute-done.6.refs_1_.refs_3_.refs_5_), channel_id=1, source_target_pairs={{1,0},{3,2},{5,4},{7,6},{9,8},{11,10},{13,12},{15,14},{17,16},{19,... | collective-permute-start | bytes 1572872 | tf_op jit(solution)/shard_map/ppermute | solution.py:185
  95.6 0.9 collective-permute-done.8
  96.5 1.3 collective-permute-start.20
  97.8 3.1 %collective-permute-start.23 = (f16[2,2,64,512]{3,2,1,0:T(8,128)(2,1)S(1)}, f16[2,2,64,512]{3,2,1,0:T(8,128)(2,1)S(1)}, u32[]{:S(2)}, u32[]{:S(2)}) collective-permute-start(f16[2,2,64,512]{3,2,1,0:T(8,128)(2,1)S(1)} %convert_element_type.287), channel_id=1, source_target_pairs={{0,4},{2,6},{4,0},{6,2},{8,12},{10,14},{12,8},{14,10},{1,5},{3,7},... | collective-permute-start | bytes 786440 | tf_op jit(solution)/shard_map/ppermute | solution.py:181
  101.0 2.6 %collective-permute-start.15 = (f16[1,2,64,512]{3,2,1,0:T(8,128)(2,1)S(1)}, f16[1,2,64,512]{3,2,1,0:T(8,128)(2,1)S(1)}, u32[]{:S(2)}, u32[]{:S(2)}) collective-permute-start(f16[1,2,64,512]{3,2,1,0:T(8,128)(2,1)S(1)} %add_convert_fusion.2), channel_id=1, source_target_pairs={{0,8},{2,10},{4,12},{6,14},{8,0},{10,2},{12,4},{14,6},{1,9},{3,11}... | collective-permute-start | bytes 393224 | tf_op jit(solution)/shard_map/ppermute | solution.py:181
  103.6 1.0 shard_map.26
  104.6 0.1 convert_element_type.282
  104.6 1.9 %collective-permute-start.21 = (f16[2,3,64,512]{3,2,1,0:T(8,128)(2,1)S(1)}, f16[2,3,64,512]{3,2,1,0:T(8,128)(2,1)S(1)}, u32[]{:S(2)}, u32[]{:S(2)}) collective-permute-start(f16[2,3,64,512]{3,2,1,0:T(8,128)(2,1)S(1)} %convert_element_type.282), channel_id=1, source_target_pairs={{0,4},{2,6},{4,0},{6,2},{8,12},{10,14},{12,8},{14,10},{16,20},{18,... | collective-permute-start | bytes 1179656 | tf_op jit(solution)/shard_map/ppermute | solution.py:182
  106.6 3.8 %collective-permute-done.23 = f16[2,2,64,512]{3,2,1,0:T(8,128)(2,1)S(1)} collective-permute-done((f16[2,2,64,512]{3,2,1,0:T(8,128)(2,1)S(1)}, f16[2,2,64,512]{3,2,1,0:T(8,128)(2,1)S(1)}, u32[]{:S(2)}, u32[]{:S(2)}) %collective-permute-start.23) | collective-permute-done | bytes 262176 | tf_op jit(solution)/shard_map/ppermute | solution.py:181
  110.4 2.4 %collective-permute-start.24 = (f16[1,2,64,512]{3,2,1,0:T(8,128)(2,1)S(1)}, f16[1,2,64,512]{3,2,1,0:T(8,128)(2,1)S(1)}, u32[]{:S(2)}, u32[]{:S(2)}) collective-permute-start(f16[1,2,64,512]{3,2,1,0:T(8,128)(2,1)S(1)} %add_convert_fusion.1), channel_id=1, source_target_pairs={{0,8},{2,10},{4,12},{6,14},{8,0},{10,2},{12,4},{14,6},{1,9},{3,11}... | collective-permute-start | bytes 393224 | tf_op jit(solution)/shard_map/ppermute | solution.py:181
  112.8 0.1 multiply_bitcast_fusion.2.refs_2_
  112.9 3.4 %collective-permute-done.21 = f16[2,3,64,512]{3,2,1,0:T(8,128)(2,1)S(1)} collective-permute-done((f16[2,3,64,512]{3,2,1,0:T(8,128)(2,1)S(1)}, f16[2,3,64,512]{3,2,1,0:T(8,128)(2,1)S(1)}, u32[]{:S(2)}, u32[]{:S(2)}) %collective-permute-start.21) | collective-permute-done | bytes 393248 | tf_op jit(solution)/shard_map/ppermute | solution.py:182
  116.3 0.1 add_convert_fusion
  116.4 4.1 %collective-permute-start.22 = (f16[1,3,64,512]{3,2,1,0:T(8,128)(2,1)S(1)}, f16[1,3,64,512]{3,2,1,0:T(8,128)(2,1)S(1)}, u32[]{:S(2)}, u32[]{:S(2)}) collective-permute-start(f16[1,3,64,512]{3,2,1,0:T(8,128)(2,1)S(1)} %add_convert_fusion), channel_id=1, source_target_pairs={{0,8},{2,10},{4,12},{6,14},{8,0},{10,2},{12,4},{14,6},{16,24},{18,... | collective-permute-start | bytes 589832 | tf_op jit(solution)/shard_map/ppermute | solution.py:182
  120.5 0.1 multiply_bitcast_fusion.1.refs_4_
  120.6 6.4 %collective-permute-done.22 = f16[1,3,64,512]{3,2,1,0:T(8,128)(2,1)S(1)} collective-permute-done((f16[1,3,64,512]{3,2,1,0:T(8,128)(2,1)S(1)}, f16[1,3,64,512]{3,2,1,0:T(8,128)(2,1)S(1)}, u32[]{:S(2)}, u32[]{:S(2)}) %collective-permute-start.22) | collective-permute-done | bytes 196640 | tf_op jit(solution)/shard_map/ppermute | solution.py:182
  126.9 0.1 multiply_bitcast_fusion.refs_3_
  127.0 1.2 shard_map.28.refs_1_
  128.2 0.7 shard_map.29
  (36 shorter events, 0.6 us)
Async XLA Ops:
  0.0 1.6 %copy-start = (bf16[512,2048]{1,0:T(8,128)(2,1)S(1)}, bf16[512,2048]{1,0:T(8,128)(2,1)}, u32[]{:S(2)}) copy-start(bf16[512,2048]{1,0:T(8,128)(2,1)} %d_ref.1) | copy-start | bytes 6291460
  2.2 4.7 %collective-permute-start = (f32[4,512]{1,0:T(4,128)S(1)}, f32[4,512]{1,0:T(4,128)S(1)}, u32[]{:S(2)}, u32[]{:S(2)}) collective-permute-start(f32[4,512]{1,0:T(4,128)S(1)} %get-tuple-element.34), channel_id=1, source_target_pairs={{0,2},{2,0},{4,6},{6,4},{8,10},{10,8},{12,14},{14,12},{1,3},{3,1},... | collective-permute-start | bytes 24584 | tf_op jit(solution)/shard_map/ppermute | solution.py:181
  6.9 3.7 %collective-permute-start.1 = (f32[4,512]{1,0:T(4,128)S(1)}, f32[4,512]{1,0:T(4,128)S(1)}, u32[]{:S(2)}, u32[]{:S(2)}) collective-permute-start(f32[4,512]{1,0:T(4,128)S(1)} %add.203), channel_id=1, source_target_pairs={{0,4},{2,6},{4,0},{6,2},{8,12},{10,14},{12,8},{14,10},{1,5},{3,7},... | collective-permute-start | bytes 24584 | tf_op jit(solution)/shard_map/ppermute | solution.py:181
  10.6 4.7 %collective-permute-start.2 = (f32[4,512]{1,0:T(4,128)S(1)}, f32[4,512]{1,0:T(4,128)S(1)}, u32[]{:S(2)}, u32[]{:S(2)}) collective-permute-start(f32[4,512]{1,0:T(4,128)S(1)} %add.204.a_ref), channel_id=1, source_target_pairs={{0,8},{2,10},{4,12},{6,14},{8,0},{10,2},{12,4},{14,6},{1,9},{3,11}... | collective-permute-start | bytes 24584 | tf_op jit(solution)/shard_map/ppermute | solution.py:181
  16.6 7.8 %collective-permute-start.9 = (f16[2,2,64,512]{3,2,1,0:T(8,128)(2,1)S(1)}, f16[2,2,64,512]{3,2,1,0:T(8,128)(2,1)S(1)}, u32[]{:S(2)}, u32[]{:S(2)}) collective-permute-start(f16[2,2,64,512]{3,2,1,0:T(8,128)(2,1)S(1)} %convert_element_type.262), channel_id=1, source_target_pairs={{0,4},{2,6},{4,0},{6,2},{8,12},{10,14},{12,8},{14,10},{1,5},{3,7},... | collective-permute-start | bytes 786440 | tf_op jit(solution)/shard_map/ppermute | solution.py:181
  18.6 15.2 %collective-permute-start.6 = (bf16[512,512]{1,0:T(8,128)(2,1)S(1)}, bf16[512,512]{1,0:T(8,128)(2,1)S(1)}, u32[]{:S(2)}, u32[]{:S(2)}) collective-permute-start(bf16[512,512]{1,0:T(8,128)(2,1)S(1)} %get-tuple-element.37.refs_0_.refs_1_.refs_2_), channel_id=1, source_target_pairs={{0,2},{2,0},{4,6},{6,4},{8,10},{10,8},{12,14},{14,12},{1,3},{3,1},... | collective-permute-start | bytes 1572872 | tf_op jit(solution)/shard_map/ppermute | solution.py:181
  24.5 7.3 %collective-permute-start.10 = (f16[1,2,64,512]{3,2,1,0:T(8,128)(2,1)S(1)}, f16[1,2,64,512]{3,2,1,0:T(8,128)(2,1)S(1)}, u32[]{:S(2)}, u32[]{:S(2)}) collective-permute-start(f16[1,2,64,512]{3,2,1,0:T(8,128)(2,1)S(1)} %add_convert_fusion.3), channel_id=1, source_target_pairs={{0,8},{2,10},{4,12},{6,14},{8,0},{10,2},{12,4},{14,6},{1,9},{3,11}... | collective-permute-start | bytes 393224 | tf_op jit(solution)/shard_map/ppermute | solution.py:181
  27.5 42.0 %collective-permute-start.3 = (bf16[512,512]{1,0:T(8,128)(2,1)S(1)}, bf16[512,512]{1,0:T(8,128)(2,1)S(1)}, u32[]{:S(2)}, u32[]{:S(2)}) collective-permute-start(bf16[512,512]{1,0:T(8,128)(2,1)S(1)} %get-tuple-element.40.refs_3_.refs_0_.own), channel_id=1, source_target_pairs={{0,2},{2,0},{4,6},{6,4},{8,10},{10,8},{12,14},{14,12},{1,3},{3,1},... | collective-permute-start | bytes 1572872 | tf_op jit(solution)/shard_map/ppermute | solution.py:181
  29.0 37.4 %collective-permute-start.4 = (bf16[512,512]{1,0:T(8,128)(2,1)S(1)}, bf16[512,512]{1,0:T(8,128)(2,1)S(1)}, u32[]{:S(2)}, u32[]{:S(2)}) collective-permute-start(bf16[512,512]{1,0:T(8,128)(2,1)S(1)} %get-tuple-element.39.refs_2_.refs_0_.refs_1_), channel_id=1, source_target_pairs={{0,2},{2,0},{4,6},{6,4},{8,10},{10,8},{12,14},{14,12},{1,3},{3,1},... | collective-permute-start | bytes 1572872 | tf_op jit(solution)/shard_map/ppermute | solution.py:181
  29.5 34.6 %collective-permute-start.5 = (bf16[512,512]{1,0:T(8,128)(2,1)S(1)}, bf16[512,512]{1,0:T(8,128)(2,1)S(1)}, u32[]{:S(2)}, u32[]{:S(2)}) collective-permute-start(bf16[512,512]{1,0:T(8,128)(2,1)S(1)} %get-tuple-element.38.refs_1_.refs_0_.refs_2_), channel_id=1, source_target_pairs={{0,2},{2,0},{4,6},{6,4},{8,10},{10,8},{12,14},{14,12},{1,3},{3,1},... | collective-permute-start | bytes 1572872 | tf_op jit(solution)/shard_map/ppermute | solution.py:181
  31.9 31.8 %collective-permute-start.11 = (f16[1,64,512]{2,1,0:T(8,128)(2,1)S(1)}, f16[1,64,512]{2,1,0:T(8,128)(2,1)S(1)}, u32[]{:S(2)}, u32[]{:S(2)}) collective-permute-start(f16[1,64,512]{2,1,0:T(8,128)(2,1)S(1)} %fusion.1), channel_id=1, source_target_pairs={{0,2},{2,0},{4,6},{6,4},{8,10},{10,8},{12,14},{14,12},{1,3},{3,1},... | collective-permute-start | bytes 196616 | tf_op jit(solution)/shard_map/ppermute | solution.py:181
  33.8 67.2 %collective-permute-start.17 = (bf16[512,512]{1,0:T(8,128)(2,1)S(1)}, bf16[512,512]{1,0:T(8,128)(2,1)S(1)}, u32[]{:S(2)}, u32[]{:S(2)}) collective-permute-start(bf16[512,512]{1,0:T(8,128)(2,1)S(1)} %get-tuple-element.37.refs_0_.refs_1_.refs_2_), channel_id=1, source_target_pairs={{1,0},{3,2},{5,4},{7,6},{9,8},{11,10},{13,12},{15,14},{17,16},{19,... | collective-permute-start | bytes 1572872 | tf_op jit(solution)/shard_map/ppermute | solution.py:185
  63.6 7.5 %collective-permute-start.12 = (f16[2,1,64,512]{3,2,1,0:T(8,128)(2,1)S(1)}, f16[2,1,64,512]{3,2,1,0:T(8,128)(2,1)S(1)}, u32[]{:S(2)}, u32[]{:S(2)}) collective-permute-start(f16[2,1,64,512]{3,2,1,0:T(8,128)(2,1)S(1)} %convert_element_type.272), channel_id=1, source_target_pairs={{0,4},{2,6},{4,0},{6,2},{8,12},{10,14},{12,8},{14,10},{1,5},{3,7},... | collective-permute-start | bytes 393224 | tf_op jit(solution)/shard_map/ppermute | solution.py:181
  64.1 28.9 %collective-permute-start.16 = (f32[2,512]{1,0:T(2,128)S(1)}, f32[2,512]{1,0:T(2,128)S(1)}, u32[]{:S(2)}, u32[]{:S(2)}) collective-permute-start(f32[2,512]{1,0:T(2,128)S(1)} %get-tuple-element.54), channel_id=1, source_target_pairs={{1,0},{3,2},{5,4},{7,6},{9,8},{11,10},{13,12},{15,14},{17,16},{19,... | collective-permute-start | bytes 12296 | tf_op jit(solution)/shard_map/ppermute | solution.py:185
  66.4 31.4 %collective-permute-start.14 = (f16[2,2,64,512]{3,2,1,0:T(8,128)(2,1)S(1)}, f16[2,2,64,512]{3,2,1,0:T(8,128)(2,1)S(1)}, u32[]{:S(2)}, u32[]{:S(2)}) collective-permute-start(f16[2,2,64,512]{3,2,1,0:T(8,128)(2,1)S(1)} %convert_element_type.277), channel_id=1, source_target_pairs={{0,4},{2,6},{4,0},{6,2},{8,12},{10,14},{12,8},{14,10},{1,5},{3,7},... | collective-permute-start | bytes 786440 | tf_op jit(solution)/shard_map/ppermute | solution.py:181
  69.5 8.7 %collective-permute-start.25 = (f16[2,1,64,512]{3,2,1,0:T(8,128)(2,1)S(1)}, f16[2,1,64,512]{3,2,1,0:T(8,128)(2,1)S(1)}, u32[]{:S(2)}, u32[]{:S(2)}) collective-permute-start(f16[2,1,64,512]{3,2,1,0:T(8,128)(2,1)S(1)} %convert_element_type.292), channel_id=1, source_target_pairs={{0,4},{2,6},{4,0},{6,2},{8,12},{10,14},{12,8},{14,10},{1,5},{3,7},... | collective-permute-start | bytes 393224 | tf_op jit(solution)/shard_map/ppermute | solution.py:181
  71.2 9.9 %collective-permute-start.27 = (f16[2,1,64,512]{3,2,1,0:T(8,128)(2,1)S(1)}, f16[2,1,64,512]{3,2,1,0:T(8,128)(2,1)S(1)}, u32[]{:S(2)}, u32[]{:S(2)}) collective-permute-start(f16[2,1,64,512]{3,2,1,0:T(8,128)(2,1)S(1)} %convert_element_type.297), channel_id=1, source_target_pairs={{0,4},{2,6},{4,0},{6,2},{8,12},{10,14},{12,8},{14,10},{1,5},{3,7},... | collective-permute-start | bytes 393224 | tf_op jit(solution)/shard_map/ppermute | solution.py:181
  78.3 5.8 %collective-permute-start.7 = (f16[2,1,64,512]{3,2,1,0:T(8,128)(2,1)S(1)}, f16[2,1,64,512]{3,2,1,0:T(8,128)(2,1)S(1)}, u32[]{:S(2)}, u32[]{:S(2)}) collective-permute-start(f16[2,1,64,512]{3,2,1,0:T(8,128)(2,1)S(1)} %convert_element_type.257), channel_id=1, source_target_pairs={{0,4},{2,6},{4,0},{6,2},{8,12},{10,14},{12,8},{14,10},{1,5},{3,7},... | collective-permute-start | bytes 393224 | tf_op jit(solution)/shard_map/ppermute | solution.py:181
  81.1 6.1 %collective-permute-start.13 = (f16[1,1,64,512]{3,2,1,0:T(8,128)(2,1)S(1)}, f16[1,1,64,512]{3,2,1,0:T(8,128)(2,1)S(1)}, u32[]{:S(2)}, u32[]{:S(2)}) collective-permute-start(f16[1,1,64,512]{3,2,1,0:T(8,128)(2,1)S(1)} %add_convert_fusion.6), channel_id=1, source_target_pairs={{0,8},{2,10},{4,12},{6,14},{8,0},{10,2},{12,4},{14,6},{1,9},{3,11}... | collective-permute-start | bytes 196616 | tf_op jit(solution)/shard_map/ppermute | solution.py:181
  84.1 6.5 %collective-permute-start.26 = (f16[1,1,64,512]{3,2,1,0:T(8,128)(2,1)S(1)}, f16[1,1,64,512]{3,2,1,0:T(8,128)(2,1)S(1)}, u32[]{:S(2)}, u32[]{:S(2)}) collective-permute-start(f16[1,1,64,512]{3,2,1,0:T(8,128)(2,1)S(1)} %add_convert_fusion.5), channel_id=1, source_target_pairs={{0,8},{2,10},{4,12},{6,14},{8,0},{10,2},{12,4},{14,6},{1,9},{3,11}... | collective-permute-start | bytes 196616 | tf_op jit(solution)/shard_map/ppermute | solution.py:181
  87.2 7.1 %collective-permute-start.28 = (f16[1,1,64,512]{3,2,1,0:T(8,128)(2,1)S(1)}, f16[1,1,64,512]{3,2,1,0:T(8,128)(2,1)S(1)}, u32[]{:S(2)}, u32[]{:S(2)}) collective-permute-start(f16[1,1,64,512]{3,2,1,0:T(8,128)(2,1)S(1)} %add_convert_fusion.4), channel_id=1, source_target_pairs={{0,8},{2,10},{4,12},{6,14},{8,0},{10,2},{12,4},{14,6},{1,9},{3,11}... | collective-permute-start | bytes 196616 | tf_op jit(solution)/shard_map/ppermute | solution.py:181
  90.6 5.8 %collective-permute-start.8 = (f16[1,1,64,512]{3,2,1,0:T(8,128)(2,1)S(1)}, f16[1,1,64,512]{3,2,1,0:T(8,128)(2,1)S(1)}, u32[]{:S(2)}, u32[]{:S(2)}) collective-permute-start(f16[1,1,64,512]{3,2,1,0:T(8,128)(2,1)S(1)} %add_convert_fusion.8), channel_id=1, source_target_pairs={{0,8},{2,10},{4,12},{6,14},{8,0},{10,2},{12,4},{14,6},{1,9},{3,11}... | collective-permute-start | bytes 196616 | tf_op jit(solution)/shard_map/ppermute | solution.py:181
  93.0 10.6 %collective-permute-start.18 = (bf16[512,512]{1,0:T(8,128)(2,1)S(1)}, bf16[512,512]{1,0:T(8,128)(2,1)S(1)}, u32[]{:S(2)}, u32[]{:S(2)}) collective-permute-start(bf16[512,512]{1,0:T(8,128)(2,1)S(1)} %get-tuple-element.38.refs_1_.refs_0_.refs_2_), channel_id=1, source_target_pairs={{1,0},{3,2},{5,4},{7,6},{9,8},{11,10},{13,12},{15,14},{17,16},{19,... | collective-permute-start | bytes 1572872 | tf_op jit(solution)/shard_map/ppermute | solution.py:185
  94.3 9.3 %collective-permute-start.19 = (bf16[512,512]{1,0:T(8,128)(2,1)S(1)}, bf16[512,512]{1,0:T(8,128)(2,1)S(1)}, u32[]{:S(2)}, u32[]{:S(2)}) collective-permute-start(bf16[512,512]{1,0:T(8,128)(2,1)S(1)} %collective-permute-done.6.refs_1_.refs_3_.refs_5_), channel_id=1, source_target_pairs={{1,0},{3,2},{5,4},{7,6},{9,8},{11,10},{13,12},{15,14},{17,16},{19,... | collective-permute-start | bytes 1572872 | tf_op jit(solution)/shard_map/ppermute | solution.py:185
  96.5 7.1 %collective-permute-start.20 = (bf16[512,512]{1,0:T(8,128)(2,1)S(1)}, bf16[512,512]{1,0:T(8,128)(2,1)S(1)}, u32[]{:S(2)}, u32[]{:S(2)}) collective-permute-start(bf16[512,512]{1,0:T(8,128)(2,1)S(1)} %collective-permute-done.5.refs_2_.refs_3_.refs_5_.refs_4_), channel_id=1, source_target_pairs={{1,0},{3,2},{5,4},{7,6},{9,8},{11,10},{13,12},{15,14},{17,16},{19,... | collective-permute-start | bytes 1572872 | tf_op jit(solution)/shard_map/ppermute | solution.py:185
  97.8 12.5 %collective-permute-start.23 = (f16[2,2,64,512]{3,2,1,0:T(8,128)(2,1)S(1)}, f16[2,2,64,512]{3,2,1,0:T(8,128)(2,1)S(1)}, u32[]{:S(2)}, u32[]{:S(2)}) collective-permute-start(f16[2,2,64,512]{3,2,1,0:T(8,128)(2,1)S(1)} %convert_element_type.287), channel_id=1, source_target_pairs={{0,4},{2,6},{4,0},{6,2},{8,12},{10,14},{12,8},{14,10},{1,5},{3,7},... | collective-permute-start | bytes 786440 | tf_op jit(solution)/shard_map/ppermute | solution.py:181
  101.0 11.8 %collective-permute-start.15 = (f16[1,2,64,512]{3,2,1,0:T(8,128)(2,1)S(1)}, f16[1,2,64,512]{3,2,1,0:T(8,128)(2,1)S(1)}, u32[]{:S(2)}, u32[]{:S(2)}) collective-permute-start(f16[1,2,64,512]{3,2,1,0:T(8,128)(2,1)S(1)} %add_convert_fusion.2), channel_id=1, source_target_pairs={{0,8},{2,10},{4,12},{6,14},{8,0},{10,2},{12,4},{14,6},{1,9},{3,11}... | collective-permute-start | bytes 393224 | tf_op jit(solution)/shard_map/ppermute | solution.py:181
  104.6 11.7 %collective-permute-start.21 = (f16[2,3,64,512]{3,2,1,0:T(8,128)(2,1)S(1)}, f16[2,3,64,512]{3,2,1,0:T(8,128)(2,1)S(1)}, u32[]{:S(2)}, u32[]{:S(2)}) collective-permute-start(f16[2,3,64,512]{3,2,1,0:T(8,128)(2,1)S(1)} %convert_element_type.282), channel_id=1, source_target_pairs={{0,4},{2,6},{4,0},{6,2},{8,12},{10,14},{12,8},{14,10},{16,20},{18,... | collective-permute-start | bytes 1179656 | tf_op jit(solution)/shard_map/ppermute | solution.py:182
  110.4 10.1 %collective-permute-start.24 = (f16[1,2,64,512]{3,2,1,0:T(8,128)(2,1)S(1)}, f16[1,2,64,512]{3,2,1,0:T(8,128)(2,1)S(1)}, u32[]{:S(2)}, u32[]{:S(2)}) collective-permute-start(f16[1,2,64,512]{3,2,1,0:T(8,128)(2,1)S(1)} %add_convert_fusion.1), channel_id=1, source_target_pairs={{0,8},{2,10},{4,12},{6,14},{8,0},{10,2},{12,4},{14,6},{1,9},{3,11}... | collective-permute-start | bytes 393224 | tf_op jit(solution)/shard_map/ppermute | solution.py:181
  116.4 10.6 %collective-permute-start.22 = (f16[1,3,64,512]{3,2,1,0:T(8,128)(2,1)S(1)}, f16[1,3,64,512]{3,2,1,0:T(8,128)(2,1)S(1)}, u32[]{:S(2)}, u32[]{:S(2)}) collective-permute-start(f16[1,3,64,512]{3,2,1,0:T(8,128)(2,1)S(1)} %add_convert_fusion), channel_id=1, source_target_pairs={{0,8},{2,10},{4,12},{6,14},{8,0},{10,2},{12,4},{14,6},{16,24},{18,... | collective-permute-start | bytes 589832 | tf_op jit(solution)/shard_map/ppermute | solution.py:182
